TPU v7x, 32 devices: a whole 2x2x4 slice. The times are simulated.
32 devices in a mesh: segment: 4 (over y, x), chan: 8 (over z, core).
Axes of the slice: x: 2, y: 2, z: 4, core: 2. Of those that a mesh axis runs over, the one named last changes fastest.
Arguments:
- resident: float32 [4, 1280, 512], P('segment', 'chan'), may hold values from -6 to 6
- held_skip: float32 [4, 1280, 512], P('segment', 'chan'), may hold values from -6 to 6
- fresh: float32 [2, 1280, 512], P(None, 'chan'), may hold values from -6 to 6
- first_weight: float32 [4, 1280, 11520], P('segment', 'chan'), may hold values from -0.0546875 to 0.0546875
- second_weight: float32 [4, 1280, 11520], P('segment', 'chan'), may hold values from -0.0546875 to 0.0546875
Outputs:
- last_outputs: float32 [4, 1280, 512], P('segment', 'chan')
All inputs are finite; a program needn't handle non-finite values.
Results may differ from a plain program's by a relative error of at most 0.0001.
Values sent between devices are 32-bit elements; how exact they have to be, the bound alone decides.
A program may use at most 128 MiB of HBM per device.

v0:
```python
import functools

import jax
import jax.numpy as jnp
from jax import lax
from jax.experimental import pallas as pl
from jax.experimental.pallas import tpu as pltpu
from jax.sharding import PartitionSpec as P

ROWS = 16
COLS = 32
MESH = pl.DeviceIdType.MESH


def silu(v):
    return v / (1.0 + jnp.exp(-v))


def block_of(rows):
    for size in (32, 40, 16):
        if rows % size == 0:
            return size
    return 8


HALVES = 2


def kernel(
    segments, n, ticks,
    resident, held_skip, fresh, first_weight, second_weight, out_ref,
    stage, wv, g, operand, acc, conv_first, passed_out,
    w_sem, recv_sem, send_sem, pass_send, pass_recv,
):
    seg = lax.axis_index("segment")
    me = lax.axis_index("chan")
    place = me // 2
    core = me % 2
    partner = me + 1 - 2 * core
    length = n // 2
    half = segments // 2
    encoder = seg < half
    shares_input = seg == half
    rows, positions = resident.shape
    part_positions = positions // HALVES
    width = 2 * rows
    channels = length * width
    blk = block_of(rows)
    split_blk = 32 if rows % 32 == 0 else rows

    def load(conv, tap):
        source = (first_weight, second_weight)[conv]
        columns = pl.ds(pl.multiple_of(tap * channels, 128), channels)
        return pltpu.make_async_copy(source.at[0, :, columns], stage.at[tap], w_sem.at[tap])

    def start_loads(conv):
        def one(tap, _):
            load(conv, tap).start()
            return 0
        lax.fori_loop(0, 9, one, 0)

    def split_weights(conv):
        def three_taps(y, _):
            for x in range(3):
                tap = 3 * y + x
                load(conv, tap).wait()

                def some_rows(i, _):
                    start = i * split_blk
                    if split_blk != rows:
                        start = pl.multiple_of(start, 16)
                    for q in range(length):
                        value = stage[tap, pl.ds(start, split_blk), q * width : (q + 1) * width]
                        high = value.astype(jnp.bfloat16)
                        low = (value - high.astype(jnp.float32)).astype(jnp.bfloat16)
                        spot = pl.ds(x * rows + start, split_blk)
                        if split_blk != rows:
                            spot = pl.ds(pl.multiple_of(x * rows + start, 16), split_blk)
                        wv[conv, q, y, spot, 0:width] = high
                        wv[conv, q, y, spot, width : 2 * width] = low
                        wv[conv, q, y, spot, 2 * width : 3 * width] = high
                    return 0
                if split_blk == rows:
                    some_rows(0, 0)
                else:
                    lax.fori_loop(0, rows // split_blk, some_rows, 0)
            return 0
        lax.fori_loop(0, 3, three_taps, 0)

    start_loads(0)

    barrier = pltpu.get_barrier_semaphore()

    def greet(cond, segment, chan):
        @pl.when(cond)
        def _():
            pl.semaphore_signal(barrier, inc=1, device_id=(segment, chan), device_id_type=MESH)
        return jnp.where(cond, 1, 0)

    greeted = greet(place > 0, seg, jnp.maximum(me - 2, 0))
    greeted += greet(place < length - 1, seg, jnp.minimum(me + 2, n - 1))
    greeted += greet(place >= 0, seg, partner)
    greeted += greet(seg > 0, jnp.maximum(seg - 1, 0), me)
    greeted += greet(seg < segments - 1, jnp.minimum(seg + 1, segments - 1), me)
    greeted += greet(seg >= 0, segments - 1 - seg, me)
    pl.semaphore_wait(barrier, greeted)

    def hop(k, j, h, way):
        target = (jnp.maximum(me - 2, 0), jnp.minimum(me + 2, n - 1), partner)[way]
        return pltpu.make_async_remote_copy(
            src_ref=g.at[k, j, h],
            dst_ref=g.at[k, j, h],
            send_sem=send_sem.at[k % 2, way, j, h],
            recv_sem=recv_sem.at[k, j, h],
            device_id=(seg, target),
            device_id_type=MESH,
        )

    def give(t, kind, h):
        target = (jnp.minimum(seg + 1, segments - 1), segments - 1 - seg)[kind]
        return pltpu.make_async_remote_copy(
            src_ref=passed_out.at[t, h],
            dst_ref=g.at[2 * (t + 1) + kind, me, h],
            send_sem=pass_send.at[t, kind, h],
            recv_sem=pass_recv.at[t, kind, h],
            device_id=(target, me),
            device_id_type=MESH,
        )

    def multiply(k, conv, q, h, first):
        for i in range(2):
            part = g[k, 2 * q + i, h]
            high = part.astype(jnp.bfloat16)
            low = (part - high.astype(jnp.float32)).astype(jnp.bfloat16)
            operand[i * rows : (i + 1) * rows] = high
            operand[width + i * rows : width + (i + 1) * rows] = high
            operand[2 * width + i * rows : 2 * width + (i + 1) * rows] = low

        def group(m, _):
            product = jnp.dot(
                wv[conv, q, m], operand[...], preferred_element_type=jnp.float32
            )
            if first:
                acc[h, m] = product
            else:
                acc[h, m] += product
            return 0
        lax.fori_loop(0, 3, group, 0)

    def drain(k):
        def one(u, _):
            q = u // HALVES
            h = u % HALVES
            j = 2 * q + core
            hop(k, j, h, 2).wait_send()

            @pl.when((q <= place) & (place < length - 1))
            def _():
                hop(k, j, h, 1).wait_send()

            @pl.when((q >= place) & (place > 0))
            def _():
                hop(k, j, h, 0).wait_send()
            return 0
        lax.fori_loop(0, length * HALVES, one, 0)

    def gather_and_multiply(k, conv, ready):
        if k >= 2:
            drain(k - 2)
        for h in range(HALVES):
            ready(h)

            @pl.when(place < length - 1)
            def _():
                hop(k, me, h, 1).start()

            @pl.when(place > 0)
            def _():
                hop(k, me, h, 0).start()

            hop(k, me, h, 2).start()

        if k < 2:
            split_weights(conv)
            if conv == 0:
                start_loads(1)

        def own(h, _):
            hop(k, partner, h, 2).wait_recv()
            multiply(k, conv, place, h, True)
            return 0
        lax.fori_loop(0, HALVES, own, 0)

        inner = jnp.where(place < length // 2, 1, -1)

        def step(u, _):
            d = u // (2 * HALVES) + 1
            turn = (u // HALVES) % 2
            h = u % HALVES
            way = jnp.where(turn == 0, inner, -inner)
            q = place + way * d
            mine = 2 * q + core

            @pl.when((q >= 0) & (q < length))
            def _():
                hop(k, mine, h, 2).wait_recv()

                @pl.when((way > 0) & (place > 0))
                def _():
                    hop(k, mine, h, 0).start()

                @pl.when((way < 0) & (place < length - 1))
                def _():
                    hop(k, mine, h, 1).start()
                hop(k, mine, h, 2).start()
                hop(k, 2 * q + 1 - core, h, 2).wait_recv()
                multiply(k, conv, q, h, False)
            return 0
        lax.fori_loop(0, (length - 1) * 2 * HALVES, step, 0)

    def multiply_held(k, conv):
        for h in range(HALVES):
            multiply(k, conv, 0, h, True)

        def one(u, _):
            multiply(k, conv, u // HALVES, u % HALVES, False)
            return 0
        lax.fori_loop(HALVES, length * HALVES, one, 0)

    spot = lax.broadcasted_iota(jnp.int32, (blk, positions), 1)
    column = spot % COLS

    def placed(start):
        total = None
        for dx in (-1, 0, 1):
            column_sum = None
            for dy in (-1, 0, 1):
                at = pl.ds(pl.multiple_of((dx + 1) * rows + start, 8), blk)
                part = jnp.concatenate([acc[h, dy + 1, at, :] for h in range(HALVES)], axis=1)
                if dy:
                    part = pltpu.roll(part, (-dy * COLS) % positions, 1)
                    source = spot + dy * COLS
                    part = jnp.where((source >= 0) & (source < positions), part, 0.0)
                column_sum = part if column_sum is None else column_sum + part
            if dx:
                column_sum = pltpu.roll(column_sum, (-dx) % positions, 1)
                source = column + dx
                column_sum = jnp.where((source >= 0) & (source < COLS), column_sum, 0.0)
            total = column_sum if total is None else total + column_sum
        return total

    def over_rows(action):
        def one(i, _):
            start = pl.multiple_of(i * blk, 8)
            action(start, pl.ds(start, blk))
            return 0
        lax.fori_loop(0, rows // blk, one, 0)

    def halves_of(value):
        return [value[:, h * part_positions : (h + 1) * part_positions] for h in range(HALVES)]

    def nothing(h):
        pass

    for h in range(HALVES):
        cut = slice(h * part_positions, (h + 1) * part_positions)
        g[0, me, h] = resident[:, cut]

        @pl.when(jnp.logical_not(encoder))
        def _():
            g[1, me, h] = held_skip[:, cut]

    for t in range(ticks):
        k = 2 * t

        def input_ready(h):
            if t == 0:
                return

            @pl.when(seg > 0)
            def _():
                give(t - 1, 0, h).wait_recv()

            @pl.when(seg == 0)
            def _():
                g[k, me, h] = fresh[t - 1, :, h * part_positions : (h + 1) * part_positions]

        gather_and_multiply(k, 0, input_ready)

        def after_first(start, rows_of):
            value = placed(start)
            conv_first[rows_of, :] = value

            @pl.when(encoder)
            def _():
                for h, part in enumerate(halves_of(silu(value))):
                    g[k + 1, me, h, rows_of, :] = part
        over_rows(after_first)

        if t == 0:
            gather_and_multiply(1, 1, nothing)
        else:
            def operand_ready(h):
                @pl.when(jnp.logical_not(encoder))
                def _():
                    give(t - 1, 1, h).wait_recv()

            @pl.when(shares_input)
            def _():
                if t == 1:
                    drain(1)
                multiply_held(k, 1)

            @pl.when(jnp.logical_not(shares_input))
            def _():
                gather_and_multiply(k + 1, 1, operand_ready)

        def after_second(start, rows_of):
            value = placed(start)

            @pl.when(encoder)
            def _():
                for h, part in enumerate(halves_of(value)):
                    passed_out[t, h, rows_of, :] = g[k, me, h, rows_of, :] + part

            @pl.when(jnp.logical_not(encoder))
            def _():
                for h, part in enumerate(halves_of(silu(conv_first[rows_of, :] + value))):
                    passed_out[t, h, rows_of, :] = part
        over_rows(after_second)

        if t < ticks - 1:
            @pl.when(seg < segments - 1)
            def _():
                for h in range(HALVES):
                    give(t, 0, h).start()

            @pl.when(seg < half - 1)
            def _():
                for h in range(HALVES):
                    give(t, 1, h).start()

    drain(2 * ticks - 2)

    @pl.when(jnp.logical_not(shares_input) | (ticks == 1))
    def _():
        drain(2 * ticks - 1)

    for t in range(ticks - 1):
        for h in range(HALVES):
            @pl.when(seg < segments - 1)
            def _():
                give(t, 0, h).wait_send()

            @pl.when(seg < half - 1)
            def _():
                give(t, 1, h).wait_send()
    for h in range(HALVES):
        out_ref[:, h * part_positions : (h + 1) * part_positions] = passed_out[ticks - 1, h]


def body(segments, n, resident, held_skip, fresh, first_weight, second_weight):
    ticks = fresh.shape[0] + 1
    rows, positions = resident.shape[1:]
    part_positions = positions // HALVES
    length = n // 2
    width = 2 * rows
    vmem = pl.BlockSpec(memory_space=pltpu.VMEM)
    anywhere = pl.BlockSpec(memory_space=pl.ANY)
    out = pl.pallas_call(
        functools.partial(kernel, segments, n, ticks),
        out_shape=jax.ShapeDtypeStruct((rows, positions), jnp.float32),
        in_specs=[vmem, vmem, vmem, anywhere, anywhere],
        out_specs=vmem,
        scratch_shapes=[
            pltpu.VMEM((9, rows, length * width), jnp.float32),
            pltpu.VMEM((2, length, 3, 3 * rows, 3 * width), jnp.bfloat16),
            pltpu.VMEM((2 * ticks, n, HALVES, rows, part_positions), jnp.float32),
            pltpu.VMEM((3 * width, part_positions), jnp.bfloat16),
            pltpu.VMEM((HALVES, 3, 3 * rows, part_positions), jnp.float32),
            pltpu.VMEM((rows, positions), jnp.float32),
            pltpu.VMEM((ticks, HALVES, rows, part_positions), jnp.float32),
            pltpu.SemaphoreType.DMA((9,)),
            pltpu.SemaphoreType.DMA((2 * ticks, n, HALVES)),
            pltpu.SemaphoreType.DMA((2, 3, n, HALVES)),
            pltpu.SemaphoreType.DMA((ticks - 1, 2, HALVES)),
            pltpu.SemaphoreType.DMA((ticks - 1, 2, HALVES)),
        ],
        compiler_params=pltpu.CompilerParams(
            collective_id=0, has_side_effects=True, vmem_limit_bytes=62 * 1024 * 1024
        ),
    )(resident[0], held_skip[0], fresh, first_weight, second_weight)
    return out[None]


def solution(mesh):
    return jax.shard_map(
        functools.partial(body, mesh.shape["segment"], mesh.shape["chan"]),
        mesh=mesh,
        in_specs=(
            P("segment", "chan", None),
            P("segment", "chan", None),
            P(None, "chan", None),
            P("segment", "chan", None),
            P("segment", "chan", None),
        ),
        out_specs=P("segment", "chan", None),
        check_vma=False,
    )
```

profile of v0, /device:TPU:3, one launch (start us, length us, event | category | flops | bytes accessed | tf_op | source)
XLA Modules:
  0.0 170.6 jit_solution(7124331378782407069)
XLA Ops:
  0.0 168.9 %shard_map.55 = f32[160,512]{1,0:T(8,128)} custom-call(f32[160,512]{1,0:T(8,128)} %bitcast.4, f32[160,512]{1,0:T(8,128)} %bitcast.5, f32[2,160,512]{2,1,0:T(8,128)} %fresh.1, f32[1,160,11520]{2,1,0:T(8,128)} %first_weight.1, f32[1,160,11520]{2,1,0:T(8,128)} %second_weight.1), custom_call_target="tpu_custom_call" | custom-call | tf_op jit(solution)/shard_map/pallas_call | solution.py:370
  168.9 1.7 %copy.7 = f32[1,160,512]{2,1,0:T(8,128)} copy(f32[1,160,512]{2,1,0:T(8,128)} %bitcast.3) | data formatting | bytes 655360
where the time goes:
time: 171 us
  Pallas kernels  169 us (99%)
  local copies, waits for them, and re-layouts  1.72 us (1%)
    pallas_call x1, Pallas kernels, body(): pl.pallas_call(functools.partial(kernel, segments, n, ticks), out_shape=j...  169 us

commit v1 on v0

v1 whole, which is shorter than its diff:
```python
import functools

import jax
import jax.numpy as jnp
from jax import lax
from jax.experimental import pallas as pl
from jax.experimental.pallas import tpu as pltpu
from jax.sharding import PartitionSpec as P

ROWS = 16
COLS = 32
MESH = pl.DeviceIdType.MESH
HALVES = 2
PIECES = 2
CHUNKS = HALVES * PIECES
UNITS = 8
OWN_UNITS = 6
PARTS = ((0, UNITS // 2), (UNITS // 2, OWN_UNITS), (OWN_UNITS, UNITS))


def silu(v):
    return v / (1.0 + jnp.exp(-v))


def block_of(rows):
    for size in (32, 40, 16):
        if rows % size == 0:
            return size
    return 8


def first_decoder_tick(segments, ticks):
    return max(0, ticks - segments // 2)


def kernel(
    segments, n, ticks,
    resident, held_skip, fresh, first_weight, second_weight, out_ref,
    stage, wv, g, operand, acc, passed_out,
    w_sem, recv_sem, swap_sem, partner_sem, z_sem, y_sem, pass_sem,
):
    seg = lax.axis_index("segment")
    me = lax.axis_index("chan")
    place = me // 2
    core = me % 2
    partner = me + 1 - 2 * core
    length = n // 2
    half = segments // 2
    encoder = seg < half
    decoder = jnp.logical_not(encoder)
    first_tick = first_decoder_tick(segments, ticks)
    merge = first_tick >= 1
    merged = (seg == half) & merge
    rows, positions = resident.shape
    part_positions = positions // HALVES
    piece = positions // CHUNKS
    width = 2 * rows
    channels = length * width
    blk = block_of(rows)
    split_blk = 32 if rows % 32 == 0 else rows
    up = jnp.minimum(me + 2, n - 1)
    down = jnp.maximum(me - 2, 0)
    has_up = place < length - 1
    has_down = place > 0
    twin = jnp.where(encoder, seg + half, seg - half)

    def load(conv, tap, slot):
        source = (first_weight, second_weight)[conv]
        columns = pl.ds(pl.multiple_of(tap * channels, 128), channels)
        return pltpu.make_async_copy(source.at[0, :, columns], stage.at[slot], w_sem.at[slot])

    def store_split(conv, tap, value_of):
        def some_rows(i, _):
            start = i * split_blk
            if split_blk != rows:
                start = pl.multiple_of(start, 16)
            spot = pl.ds(pl.multiple_of(tap * rows + start, 16), split_blk)
            for q in range(length):
                value = value_of(pl.ds(start, split_blk), slice(q * width, (q + 1) * width))
                high = value.astype(jnp.bfloat16)
                low = (value - high.astype(jnp.float32)).astype(jnp.bfloat16)
                wv[conv, q, spot, 0:width] = high
                wv[conv, q, spot, width : 2 * width] = low
                wv[conv, q, spot, 2 * width : 3 * width] = high
            return 0
        lax.fori_loop(0, rows // split_blk, some_rows, 0)

    depth = 4

    def start_first_loads():
        @pl.when(jnp.logical_not(merged))
        def _():
            def one(tap, _):
                load(0, tap, tap).start()
                return 0
            lax.fori_loop(0, 9, one, 0)

        if merge:
            @pl.when(merged)
            def _():
                for tap in range(depth):
                    load(0, tap, tap).start()
                    load(1, tap, depth + tap).start()

    def split_taps(conv, low, high):
        def one(tap, _):
            load(0, 0, tap).wait()
            store_split(conv, tap, lambda r, c: stage[tap, r, c])
            return 0
        lax.fori_loop(low, high, one, 0)

    def reload_taps(low, high):
        def one(tap, _):
            load(1, tap, tap).start()
            return 0
        lax.fori_loop(low, high, one, 0)

    def split_merged(low, high):
        def one(tap, _):
            a = tap % depth
            load(0, 0, a).wait()
            load(1, 0, depth + a).wait()
            store_split(0, tap, lambda r, c: stage[a, r, c] + stage[depth + a, r, c])

            @pl.when(tap + depth < 9)
            def _():
                load(0, tap + depth, a).start()
                load(1, tap + depth, depth + a).start()
            return 0
        lax.fori_loop(low, high, one, 0)

    start_first_loads()

    barrier = pltpu.get_barrier_semaphore()

    def greet(cond, segment, chan):
        @pl.when(cond)
        def _():
            pl.semaphore_signal(barrier, inc=1, device_id=(segment, chan), device_id_type=MESH)
        return jnp.where(cond, 1, 0)

    def kept(s):
        return jnp.clip(s, 0, segments - 1)

    greeted = greet(has_down, seg, down)
    greeted += greet(has_up, seg, up)
    greeted += greet(seg >= 0, seg, partner)
    greeted += greet(seg > 0, kept(seg - 1), me)
    greeted += greet(seg < segments - 1, kept(seg + 1), me)
    greeted += greet(seg >= 0, segments - 1 - seg, me)
    greeted += greet(seg >= 0, twin, me)
    greeted += greet(seg + 1 < half, kept(seg + 1 + half), me)
    greeted += greet(seg >= half + 1, kept(seg - 1 - half), me)

    def encoder_slot(t, kind):
        return 2 * t + kind

    def decoder_slot(t, kind):
        return 2 * ticks + 2 * jnp.maximum(t - first_tick, 0) + kind

    def decoder_active(s, t):
        return s + (ticks - 1 - t) <= segments - 1

    shared = (segments + half) // 2
    shares = seg == shared
    if (segments + half) % 2:
        shares = seg < 0

    unit = CHUNKS * rows // UNITS

    def units_of(u, count):
        return pl.ds(u * unit, count * unit)

    def copy(k, q, u, count, sem, target_seg, target):
        return pltpu.make_async_remote_copy(
            src_ref=g.at[k, core, q, units_of(u, count)],
            dst_ref=g.at[k, core, q, units_of(u, count)],
            send_sem=sem,
            recv_sem=recv_sem.at[k, q, u],
            device_id=(target_seg, target),
            device_id_type=MESH,
        )

    def swap(k, parity, q, part):
        low, high = PARTS[part]
        return pltpu.make_async_remote_copy(
            src_ref=g.at[k, parity, q, units_of(low, high - low)],
            dst_ref=g.at[k, parity, q, units_of(low, high - low)],
            send_sem=partner_sem.at[k],
            recv_sem=swap_sem.at[k, q, part],
            device_id=(seg, partner),
            device_id_type=MESH,
        )

    def along(k, q, u, way):
        return copy(k, q, u, 1, z_sem.at[k, way, q], seg, (down, up)[way])

    def across(k, q, u):
        return copy(k, q, u, 1, y_sem.at[k, q], twin, me)

    def arrived(k, q, u):
        copy(k, q, u, 1, y_sem.at[k, q], twin, me).wait_recv()

    def both_ways(k, u):
        @pl.when(has_up)
        def _():
            along(k, place, u, 1).start()

        @pl.when(has_down)
        def _():
            along(k, place, u, 0).start()

    def onward(k, q, u):
        @pl.when((q > place) & has_down)
        def _():
            along(k, q, u, 0).start()

        @pl.when((q < place) & has_up)
        def _():
            along(k, q, u, 1).start()

    def swap_after(k, q, u):
        for part, (low, high) in enumerate(PARTS):
            if u == high - 1:
                swap(k, core, q, part).start()

    near = jnp.minimum(place, length - 1 - place)
    inner = jnp.where(place < length // 2, 1, -1)

    def source_of(i):
        paired = i < 2 * near
        d = jnp.where(paired, i // 2 + 1, i - near + 1)
        way = jnp.where(paired & (i % 2 == 1), -inner, inner)
        return place + way * d

    def multiply(k, w, q, h):
        for i in range(2):
            for p in range(PIECES):
                part = g[k, i, q, pl.ds((PIECES * h + p) * rows, rows)]
                high = part.astype(jnp.bfloat16)
                low = (part - high.astype(jnp.float32)).astype(jnp.bfloat16)
                cut = slice(p * piece, (p + 1) * piece)
                operand[i * rows : (i + 1) * rows, cut] = high
                operand[width + i * rows : width + (i + 1) * rows, cut] = high
                operand[2 * width + i * rows : 2 * width + (i + 1) * rows, cut] = low
        acc[h] += jnp.dot(wv[w, q], operand[...], preferred_element_type=jnp.float32)

    spot = lax.broadcasted_iota(jnp.int32, (blk, positions), 1)
    column = spot % COLS

    def placed(start):
        total = None
        for dx in (-1, 0, 1):
            column_sum = None
            for dy in (-1, 0, 1):
                tap = 3 * (dy + 1) + dx + 1
                at = pl.ds(pl.multiple_of(tap * rows + start, 8), blk)
                part = jnp.concatenate([acc[h, at, :] for h in range(HALVES)], axis=1)
                if dy:
                    part = pltpu.roll(part, (-dy * COLS) % positions, 1)
                    source = spot + dy * COLS
                    part = jnp.where((source >= 0) & (source < positions), part, 0.0)
                column_sum = part if column_sum is None else column_sum + part
            if dx:
                column_sum = pltpu.roll(column_sum, (-dx) % positions, 1)
                source = column + dx
                column_sum = jnp.where((source >= 0) & (source < COLS), column_sum, 0.0)
            total = column_sum if total is None else total + column_sum
        return total

    def over_rows(action):
        def one(i, _):
            start = pl.multiple_of(i * blk, 8)
            action(start, pl.ds(start, blk))
            return 0
        lax.fori_loop(0, rows // blk, one, 0)

    def cut_of(c):
        return slice(c * piece, (c + 1) * piece)

    def rows_at(c, start=0, count=None):
        return pl.ds(c * rows + start, rows if count is None else count)

    def fill(k, source):
        for c in range(CHUNKS):
            g[k, core, place, rows_at(c)] = source[:, cut_of(c)]

    @pl.when(encoder)
    def _():
        fill(0, resident)

    if first_tick == 0:
        @pl.when(decoder)
        def _():
            fill(2 * ticks, resident)
            fill(2 * ticks + 1, held_skip)

    @pl.when((seg == 0) | (seg == half))
    def _():
        for t in range(1, ticks):
            fill(2 * t, fresh.at[t - 1])

    pl.semaphore_wait(barrier, greeted)

    def drain_along(k, low, high):
        def one(q, _):
            @pl.when(has_up & (q <= place))
            def _():
                copy(k, q, low, high - low, z_sem.at[k, 1, q], seg, up).wait_send()

            @pl.when(has_down & (q >= place))
            def _():
                copy(k, q, low, high - low, z_sem.at[k, 0, q], seg, down).wait_send()
            return 0
        lax.fori_loop(0, length, one, 0)

    def drain_partner(k):
        pltpu.make_async_remote_copy(
            src_ref=g.at[k, core], dst_ref=g.at[k, core],
            send_sem=partner_sem.at[k], recv_sem=swap_sem.at[k, 0, 0],
            device_id=(seg, partner), device_id_type=MESH,
        ).wait_send()

    def drain_across(k, q, low, high):
        copy(k, q, low, high - low, y_sem.at[k, q], twin, me).wait_send()

    def facts_of(idx):
        t = idx // 2
        kind = idx % 2
        skip_held = shares & (kind == 1) & (t > 0)
        k = jnp.where(
            encoder,
            encoder_slot(t, kind),
            jnp.where(skip_held, encoder_slot(t, 0), decoder_slot(t, kind)),
        )
        active = encoder | (decoder_active(seg, t) & jnp.logical_not(merged & (kind == 1)))
        lifts = encoder & ((kind == 1) | (t == 0))
        lends = encoder & (twin == shared) & (kind == 0) & (t > 0) & decoder_active(twin, t)
        if (segments + half) % 2:
            lends = lends & (seg < 0)
        return t, kind, k, active, lifts, lends, skip_held

    def drain(idx):
        t, kind, k, active, lifts, lends, skip_held = facts_of(idx)
        relayed = encoder_slot(t, kind)

        @pl.when(active)
        def _():
            drain_partner(k)

            @pl.when(encoder)
            def _():
                drain_along(k, 0, OWN_UNITS)

                @pl.when(lifts)
                def _():
                    drain_across(k, place, OWN_UNITS, UNITS)

                @pl.when(lends)
                def _():
                    def one(q, _):
                        drain_across(k, q, 0, OWN_UNITS)
                        return 0
                    lax.fori_loop(0, length, one, 0)

            @pl.when(decoder & jnp.logical_not(skip_held))
            def _():
                drain_along(k, 0, UNITS)

        @pl.when(decoder)
        def _():
            drain_along(relayed, OWN_UNITS, UNITS)

            def one(q, _):
                @pl.when(q != place)
                def _():
                    drain_across(relayed, q, OWN_UNITS, UNITS)
                return 0
            lax.fori_loop(0, length, one, 0)

    others = length - 1
    slots = 2 * length
    third = slots - 4

    at_end = near == 0

    def event_of(e):
        m = (e + 1) // 2
        h = jnp.where(e == 0, 0, jnp.where(e == 2 * others - 1, 1, (e + 1) % 2))
        i = jnp.where(e == 0, 0, jnp.where(e % 2 == 1, jnp.minimum(m, others - 1), e // 2 - 1))
        return jnp.where(at_end, e // 2, i), jnp.where(at_end, e % 2, h)

    def one_stage(idx, _):
        t, kind, k, active, lifts, lends, skip_held = facts_of(idx)
        relayed = encoder_slot(t, kind)
        local = jnp.where(encoder, (kind == 1) | (t == 0) | (seg == 0), t == 0)
        ahead = (seg == 0) & (kind == 0) & (t > 0)

        @pl.when(decoder)
        def _():
            for u in range(OWN_UNITS, UNITS):
                @pl.when(jnp.logical_not((seg == half) & (kind == 0) & (t > 0)))
                def _():
                    arrived(relayed, place, u)
                both_ways(relayed, u)

        @pl.when(active)
        def _():
            for u in range(UNITS):
                if u < OWN_UNITS:
                    @pl.when(jnp.logical_not(local))
                    def _():
                        arrived(k, place, u)

                    @pl.when(jnp.logical_not(ahead | skip_held))
                    def _():
                        both_ways(k, u)

                    @pl.when(lends)
                    def _():
                        across(k, place, u).start()
                else:
                    @pl.when(jnp.logical_not(local | skip_held))
                    def _():
                        arrived(k, place, u)

                    @pl.when(decoder & jnp.logical_not(skip_held))
                    def _():
                        both_ways(k, u)

                    @pl.when(lifts)
                    def _():
                        across(k, place, u).start()
                swap_after(k, place, u)

            @pl.when(encoder | (kind == 0))
            def _():
                acc[...] = jnp.zeros_like(acc)

        @pl.when(idx > 0)
        def _():
            drain(idx - 1)

        @pl.when(encoder & (idx == 0))
        def _():
            split_taps(0, 0, 9)
            reload_taps(0, 9)

        def one_slot(s, _):
            @pl.when(decoder & (s >= 1) & (s < length))
            def _():
                q = source_of(s - 1)
                for u in range(OWN_UNITS, UNITS):
                    arrived(relayed, q, u)
                    onward(relayed, q, u)
                    across(relayed, q, u).start()

            e, part = event_of(jnp.maximum(s - 1, 0))
            gathers = active & (s >= 1) & (s <= 2 * others)

            @pl.when(gathers & (part == 0))
            def _():
                q = source_of(e)
                for u in range(OWN_UNITS):
                    arrived(k, q, u)

                    @pl.when(jnp.logical_not(skip_held))
                    def _():
                        onward(k, q, u)

                    @pl.when(lends)
                    def _():
                        across(k, q, u).start()
                    swap_after(k, q, u)

            @pl.when(gathers & (part == 1))
            def _():
                q = source_of(e)
                for u in range(OWN_UNITS, UNITS):
                    @pl.when(jnp.logical_not(skip_held))
                    def _():
                        arrived(k, q, u)

                    @pl.when(decoder & jnp.logical_not(skip_held))
                    def _():
                        onward(k, q, u)
                    swap_after(k, q, u)

            @pl.when((seg == 0) & (kind == 1) & (t < ticks - 1) & (s == 2 * others - 1))
            def _():
                for u in range(OWN_UNITS):
                    both_ways(k + 1, u)

            @pl.when((s >= third) & (s < third + 3))
            def _():
                low = 3 * (s - third)

                @pl.when(encoder & (idx == 0))
                def _():
                    split_taps(1, low, low + 3)

                @pl.when(decoder & jnp.logical_not(merged) & (idx == 0))
                def _():
                    split_taps(0, low, low + 3)
                    reload_taps(low, low + 3)

                @pl.when(decoder & jnp.logical_not(merged) & (idx == 1))
                def _():
                    split_taps(1, low, low + 3)

                if merge:
                    @pl.when(merged & (idx == 0))
                    def _():
                        split_merged(low, low + 3)

            @pl.when(active)
            def _():
                i, h = event_of(jnp.maximum(s - 2, 0))
                q = jnp.where(s < 2, place, source_of(i))
                h = jnp.where(s < 2, s, h)

                @pl.when(h == 0)
                def _():
                    swap(k, 1 - core, q, 0).wait_recv()

                @pl.when(h == 1)
                def _():
                    swap(k, 1 - core, q, 1).wait_recv()
                    swap(k, 1 - core, q, 2).wait_recv()
                multiply(k, kind, q, h)
            return 0
        lax.fori_loop(0, slots, one_slot, 0)

        def after(start, rows_of):
            value = placed(start)

            def put(parts):
                @pl.when(t == ticks - 1)
                def _():
                    for c in range(CHUNKS):
                        out_ref[rows_of, cut_of(c)] = parts[c]

                @pl.when(t < ticks - 1)
                def _():
                    for c in range(CHUNKS):
                        passed_out[jnp.minimum(t, ticks - 2), rows_at(c, start, blk), :] = parts[c]

            @pl.when(encoder & (kind == 0))
            def _():
                result = silu(value)
                for c in range(CHUNKS):
                    g[k + 1, core, place, rows_at(c, start, blk), :] = result[:, cut_of(c)]

            @pl.when(encoder & (kind == 1))
            def _():
                put([
                    g[k - 1, core, place, rows_at(c, start, blk), :] + value[:, cut_of(c)]
                    for c in range(CHUNKS)
                ])

            @pl.when(decoder)
            def _():
                result = silu(value)
                put([result[:, cut_of(c)] for c in range(CHUNKS)])

        ends = active & ((kind == 1) | merged)

        @pl.when(encoder | ends)
        def _():
            over_rows(after)

        @pl.when(ends & (t < ticks - 1))
        def _():
            give_all(t, True)
        return 0

    def give(t, kind, u, count):
        into_encoder = seg + 1 < half
        slot = (
            jnp.where(into_encoder, encoder_slot(t + 1, 0), decoder_slot(t + 1, 0)),
            encoder_slot(t + 1, 0),
            decoder_slot(t + 1, 1),
        )[kind]
        target = (kept(seg + 1), kept(seg + 1 + half), segments - 1 - seg)[kind]
        return pltpu.make_async_remote_copy(
            src_ref=passed_out.at[t, units_of(u, count)],
            dst_ref=g.at[slot, core, place, units_of(u, count)],
            send_sem=pass_sem.at[t, kind],
            recv_sem=recv_sem.at[slot, place, u],
            device_id=(target, me),
            device_id_type=MESH,
        )

    def give_all(t, starting):
        next_in = (seg + 1 < half) | ((seg < segments - 1) & decoder_active(seg + 1, t + 1))
        helper = seg + 1 < half
        mirror = segments - 1 - seg
        skip = encoder & decoder_active(mirror, t + 1)
        if merge:
            skip = skip & (mirror != half)
        if (segments + half) % 2 == 0:
            skip = skip & (mirror != shared)
        if starting:
            @pl.when(helper)
            def _():
                for u in range(OWN_UNITS, UNITS):
                    give(t, 1, u, 1).start()

            @pl.when(next_in)
            def _():
                for u in range(OWN_UNITS):
                    give(t, 0, u, 1).start()

            @pl.when(next_in)
            def _():
                for u in range(OWN_UNITS, UNITS):
                    give(t, 0, u, 1).start()

            @pl.when(skip)
            def _():
                for u in range(UNITS):
                    give(t, 2, u, 1).start()
        else:
            @pl.when(next_in)
            def _():
                give(t, 0, 0, UNITS).wait_send()

            @pl.when(helper)
            def _():
                give(t, 1, OWN_UNITS, UNITS - OWN_UNITS).wait_send()

            @pl.when(skip)
            def _():
                give(t, 2, 0, UNITS).wait_send()

    lax.fori_loop(0, 2 * ticks, one_stage, 0)
    drain(2 * ticks - 1)

    for t in range(ticks - 1):
        @pl.when(encoder | decoder_active(seg, t))
        def _():
            give_all(t, False)


def body(segments, n, resident, held_skip, fresh, first_weight, second_weight):
    ticks = fresh.shape[0] + 1
    rows, positions = resident.shape[1:]
    length = n // 2
    width = 2 * rows
    slots = 2 * ticks + 2 * (ticks - first_decoder_tick(segments, ticks))
    vmem = pl.BlockSpec(memory_space=pltpu.VMEM)
    anywhere = pl.BlockSpec(memory_space=pl.ANY)
    out = pl.pallas_call(
        functools.partial(kernel, segments, n, ticks),
        out_shape=jax.ShapeDtypeStruct((rows, positions), jnp.float32),
        in_specs=[vmem, vmem, vmem, anywhere, anywhere],
        out_specs=vmem,
        scratch_shapes=[
            pltpu.VMEM((9, rows, length * width), jnp.float32),
            pltpu.VMEM((2, length, 9 * rows, 3 * width), jnp.bfloat16),
            pltpu.VMEM((slots, 2, length, CHUNKS * rows, positions // CHUNKS), jnp.float32),
            pltpu.VMEM((3 * width, positions // HALVES), jnp.bfloat16),
            pltpu.VMEM((HALVES, 9 * rows, positions // HALVES), jnp.float32),
            pltpu.VMEM((ticks - 1, CHUNKS * rows, positions // CHUNKS), jnp.float32),
            pltpu.SemaphoreType.DMA((9,)),
            pltpu.SemaphoreType.DMA((slots, length, UNITS)),
            pltpu.SemaphoreType.DMA((slots, length, len(PARTS))),
            pltpu.SemaphoreType.DMA((slots,)),
            pltpu.SemaphoreType.DMA((slots, 2, length)),
            pltpu.SemaphoreType.DMA((slots, length)),
            pltpu.SemaphoreType.DMA((ticks - 1, 3)),
        ],
        compiler_params=pltpu.CompilerParams(
            collective_id=0, has_side_effects=True, vmem_limit_bytes=63 * 1024 * 1024
        ),
    )(resident[0], held_skip[0], fresh, first_weight, second_weight)
    return out[None]


def solution(mesh):
    return jax.shard_map(
        functools.partial(body, mesh.shape["segment"], mesh.shape["chan"]),
        mesh=mesh,
        in_specs=(
            P("segment", "chan", None),
            P("segment", "chan", None),
            P(None, "chan", None),
            P("segment", "chan", None),
            P("segment", "chan", None),
        ),
        out_specs=P("segment", "chan", None),
        check_vma=False,
    )
```

time: 171 us -> 156 us (0.912)
  Pallas kernels: 169 us -> 153 us
    pallas_call x1, Pallas kernels: 169 us -> 153 us  [body(): pl.pallas_call(functools.partial(kernel, segments, n, ticks), out_shape=j...]
where the time goes in v1:
time: 156 us; the launch traced here: 154 us
  Pallas kernels  153 us (98%)
  local copies, waits for them, and re-layouts  1.72 us (1%)
    pallas_call x1, Pallas kernels, body(): pl.pallas_call(functools.partial(kernel, segments, n, ticks), out_shape=j...  153 us

profile of v1, /device:TPU:3, one launch (start us, length us, event | category | flops | bytes accessed | tf_op | source)
XLA Modules:
  0.0 154.5 jit_solution(112586175966498974)
XLA Ops:
  0.0 152.7 %shard_map.55 = f32[160,512]{1,0:T(8,128)} custom-call(f32[160,512]{1,0:T(8,128)} %bitcast.4, f32[160,512]{1,0:T(8,128)} %bitcast.5, f32[2,160,512]{2,1,0:T(8,128)} %fresh.1, f32[1,160,11520]{2,1,0:T(8,128)} %first_weight.1, f32[1,160,11520]{2,1,0:T(8,128)} %second_weight.1), custom_call_target="tpu_custom_call" | custom-call | tf_op jit(solution)/shard_map/pallas_call | solution.py:653
  152.8 1.7 %copy.7 = f32[1,160,512]{2,1,0:T(8,128)} copy(f32[1,160,512]{2,1,0:T(8,128)} %bitcast.3) | data formatting | bytes 655360

commit v2 on v1

--- a/solution.py
+++ b/solution.py
@@ -14,8 +14,9 @@
 PIECES = 2
 CHUNKS = HALVES * PIECES
 UNITS = 8
-OWN_UNITS = 6
-PARTS = ((0, UNITS // 2), (UNITS // 2, OWN_UNITS), (OWN_UNITS, UNITS))
+OWN_UNITS = 5
+CUTS = sorted({0, UNITS // 2, OWN_UNITS, UNITS})
+PARTS = tuple(zip(CUTS[:-1], CUTS[1:]))
 
 
 def silu(v):
@@ -58,10 +59,6 @@
     channels = length * width
     blk = block_of(rows)
     split_blk = 32 if rows % 32 == 0 else rows
-    up = jnp.minimum(me + 2, n - 1)
-    down = jnp.maximum(me - 2, 0)
-    has_up = place < length - 1
-    has_down = place > 0
     twin = jnp.where(encoder, seg + half, seg - half)
 
     def load(conv, tap, slot):
@@ -142,13 +139,13 @@
     def kept(s):
         return jnp.clip(s, 0, segments - 1)
 
-    greeted = greet(has_down, seg, down)
-    greeted += greet(has_up, seg, up)
-    greeted += greet(seg >= 0, seg, partner)
+    greeted = greet(seg >= 0, seg, partner)
+    for p in range(length):
+        greeted += greet(place != p, seg, 2 * p + core)
+        greeted += greet(seg >= 0, twin, 2 * p + core)
     greeted += greet(seg > 0, kept(seg - 1), me)
     greeted += greet(seg < segments - 1, kept(seg + 1), me)
     greeted += greet(seg >= 0, segments - 1 - seg, me)
-    greeted += greet(seg >= 0, twin, me)
     greeted += greet(seg + 1 < half, kept(seg + 1 + half), me)
     greeted += greet(seg >= half + 1, kept(seg - 1 - half), me)
 
@@ -192,40 +189,48 @@
             device_id_type=MESH,
         )
 
-    def along(k, q, u, way):
-        return copy(k, q, u, 1, z_sem.at[k, way, q], seg, (down, up)[way])
-
     def across(k, q, u):
         return copy(k, q, u, 1, y_sem.at[k, q], twin, me)
 
     def arrived(k, q, u):
         copy(k, q, u, 1, y_sem.at[k, q], twin, me).wait_recv()
 
-    def both_ways(k, u):
-        @pl.when(has_up)
-        def _():
-            along(k, place, u, 1).start()
-
-        @pl.when(has_down)
-        def _():
-            along(k, place, u, 0).start()
-
-    def onward(k, q, u):
-        @pl.when((q > place) & has_down)
-        def _():
-            along(k, q, u, 0).start()
-
-        @pl.when((q < place) & has_up)
-        def _():
-            along(k, q, u, 1).start()
+    near = jnp.minimum(place, length - 1 - place)
+    at_end = near == 0
+    inner = jnp.where(place < length // 2, 1, -1)
+
+    def along(k, q, u, lane, target, relay):
+        target = jnp.clip(target, 0, length - 1)
+        ending = (target == 0) | (target == length - 1)
+        to = jnp.where(relay & (at_end | ending), twin, seg)
+        return copy(k, q, u, 1, z_sem.at[k, lane, q], to, 2 * target + core)
+
+    def send_near(k, u, relay):
+        along(k, place, u, 0, place + inner, relay).start()
+
+        @pl.when(jnp.logical_not(at_end))
+        def _():
+            along(k, place, u, 1, place - inner, relay).start()
+
+    def send_far(k):
+        @pl.when(at_end)
+        def _():
+            for d in range(2, length):
+                for u in range(OWN_UNITS, UNITS):
+                    along(k, place, u, 1, place + inner * d, True).start()
+
+    def twin_holds(q):
+        return (q > 0) & (q < length - 1) & jnp.logical_not(at_end)
+
+    def onward(k, q, u, relay):
+        @pl.when(twin_holds(q) if relay else jnp.logical_not(at_end))
+        def _():
+            along(k, q, u, 0, place + jnp.where(q < place, 1, -1), relay).start()
 
     def swap_after(k, q, u):
         for part, (low, high) in enumerate(PARTS):
             if u == high - 1:
                 swap(k, core, q, part).start()
-
-    near = jnp.minimum(place, length - 1 - place)
-    inner = jnp.where(place < length // 2, 1, -1)
 
     def source_of(i):
         paired = i < 2 * near
@@ -302,17 +307,32 @@
 
     pl.semaphore_wait(barrier, greeted)
 
-    def drain_along(k, low, high):
-        def one(q, _):
-            @pl.when(has_up & (q <= place))
-            def _():
-                copy(k, q, low, high - low, z_sem.at[k, 1, q], seg, up).wait_send()
-
-            @pl.when(has_down & (q >= place))
-            def _():
-                copy(k, q, low, high - low, z_sem.at[k, 0, q], seg, down).wait_send()
-            return 0
-        lax.fori_loop(0, length, one, 0)
+    def drain_along(k, low, high, relay):
+        def sent(q, lane):
+            copy(k, q, low, high - low, z_sem.at[k, lane, q], seg, partner).wait_send()
+
+        sent(place, 0)
+
+        @pl.when(at_end & relay)
+        def _():
+            if length > 2:
+                span = g.at[k, core, pl.ds(0, length - 2), units_of(low, high - low)]
+                pltpu.make_async_remote_copy(
+                    src_ref=span, dst_ref=span,
+                    send_sem=z_sem.at[k, 1, place], recv_sem=recv_sem.at[k, 0, 0],
+                    device_id=(seg, partner), device_id_type=MESH,
+                ).wait_send()
+
+        @pl.when(jnp.logical_not(at_end))
+        def _():
+            sent(place, 1)
+
+            def one(q, _):
+                @pl.when(q != place)
+                def _():
+                    sent(q, 0)
+                return 0
+            lax.fori_loop(int(relay), length - int(relay), one, 0)
 
     def drain_partner(k):
         pltpu.make_async_remote_copy(
@@ -323,6 +343,8 @@
 
     def drain_across(k, q, low, high):
         copy(k, q, low, high - low, y_sem.at[k, q], twin, me).wait_send()
+
+    twin_of = jnp.where(encoder, seg, twin)
 
     def facts_of(idx):
         t = idx // 2
@@ -334,23 +356,24 @@
             jnp.where(skip_held, encoder_slot(t, 0), decoder_slot(t, kind)),
         )
         active = encoder | (decoder_active(seg, t) & jnp.logical_not(merged & (kind == 1)))
-        lifts = encoder & ((kind == 1) | (t == 0))
+        solo = (twin_of == 0) & (idx == 2 * ticks - 1)
+        lifts = encoder & ((kind == 1) | (t == 0)) & jnp.logical_not(solo)
         lends = encoder & (twin == shared) & (kind == 0) & (t > 0) & decoder_active(twin, t)
         if (segments + half) % 2:
             lends = lends & (seg < 0)
-        return t, kind, k, active, lifts, lends, skip_held
+        return t, kind, k, active, lifts, lends, solo, skip_held
 
     def drain(idx):
-        t, kind, k, active, lifts, lends, skip_held = facts_of(idx)
+        t, kind, k, active, lifts, lends, solo, skip_held = facts_of(idx)
         relayed = encoder_slot(t, kind)
 
         @pl.when(active)
         def _():
             drain_partner(k)
 
-            @pl.when(encoder)
-            def _():
-                drain_along(k, 0, OWN_UNITS)
+            @pl.when(encoder & jnp.logical_not(solo))
+            def _():
+                drain_along(k, 0, OWN_UNITS, False)
 
                 @pl.when(lifts)
                 def _():
@@ -359,87 +382,145 @@
                 @pl.when(lends)
                 def _():
                     def one(q, _):
-                        drain_across(k, q, 0, OWN_UNITS)
+                        partly = (q == place) | twin_holds(q)
+
+                        @pl.when(partly)
+                        def _():
+                            drain_across(k, q, 0, OWN_UNITS)
+
+                        @pl.when(jnp.logical_not(partly))
+                        def _():
+                            drain_across(k, q, 0, UNITS)
                         return 0
                     lax.fori_loop(0, length, one, 0)
 
-            @pl.when(decoder & jnp.logical_not(skip_held))
-            def _():
-                drain_along(k, 0, UNITS)
-
-        @pl.when(decoder)
-        def _():
-            drain_along(relayed, OWN_UNITS, UNITS)
-
-            def one(q, _):
-                @pl.when(q != place)
-                def _():
-                    drain_across(relayed, q, OWN_UNITS, UNITS)
-                return 0
-            lax.fori_loop(0, length, one, 0)
+            @pl.when((decoder & jnp.logical_not(skip_held)) | (encoder & solo))
+            def _():
+                drain_along(k, 0, UNITS, False)
+
+        @pl.when(decoder & jnp.logical_not(solo))
+        def _():
+            drain_along(relayed, OWN_UNITS, UNITS, True)
+
+            @pl.when((seg != half) & (kind == 0) & (t > 0))
+            def _():
+                drain_across(relayed, place, OWN_UNITS, UNITS)
+
+            @pl.when(jnp.logical_not(at_end))
+            def _():
+                def one(q, _):
+                    @pl.when(q != place)
+                    def _():
+                        drain_across(relayed, q, OWN_UNITS, UNITS)
+                    return 0
+                lax.fori_loop(1, length - 1, one, 0)
 
     others = length - 1
     slots = 2 * length
     third = slots - 4
 
-    at_end = near == 0
-
     def event_of(e):
+        h = e // others
         m = (e + 1) // 2
-        h = jnp.where(e == 0, 0, jnp.where(e == 2 * others - 1, 1, (e + 1) % 2))
-        i = jnp.where(e == 0, 0, jnp.where(e % 2 == 1, jnp.minimum(m, others - 1), e // 2 - 1))
-        return jnp.where(at_end, e // 2, i), jnp.where(at_end, e % 2, h)
+        eh = jnp.where(e == 0, 0, jnp.where(e == 2 * others - 1, 1, (e + 1) % 2))
+        ei = jnp.where(e == 0, 0, jnp.where(e % 2 == 1, jnp.minimum(m, others - 1), e // 2 - 1))
+        return jnp.where(at_end, ei, e - h * others), jnp.where(at_end, eh, h)
+
+    def went_early(idx):
+        facts = facts_of(idx)
+        return (seg == half) & facts[3] & jnp.logical_not(facts[-1])
+
+    def relay_own(idx):
+        t = idx // 2
+        kind = idx % 2
+        relayed = encoder_slot(t, kind)
+        handed = (kind == 0) & (t > 0)
+        for u in range(OWN_UNITS, UNITS):
+            @pl.when(jnp.logical_not((seg == half) & handed))
+            def _():
+                arrived(relayed, place, u)
+
+            @pl.when((seg != half) & handed)
+            def _():
+                across(relayed, place, u).start()
+            send_near(relayed, u, True)
+        send_far(relayed)
+
+    def relay_others(idx):
+        relayed = encoder_slot(idx // 2, idx % 2)
+
+        def one(i, _):
+            q = source_of(i)
+
+            @pl.when(twin_holds(q))
+            def _():
+                for u in range(OWN_UNITS, UNITS):
+                    arrived(relayed, q, u)
+                    onward(relayed, q, u, True)
+                    across(relayed, q, u).start()
+            return 0
+        lax.fori_loop(0, others, one, 0)
 
     def one_stage(idx, _):
-        t, kind, k, active, lifts, lends, skip_held = facts_of(idx)
-        relayed = encoder_slot(t, kind)
+        t, kind, k, active, lifts, lends, solo, skip_held = facts_of(idx)
         local = jnp.where(encoder, (kind == 1) | (t == 0) | (seg == 0), t == 0)
-        ahead = (seg == 0) & (kind == 0) & (t > 0)
-
-        @pl.when(decoder)
-        def _():
-            for u in range(OWN_UNITS, UNITS):
-                @pl.when(jnp.logical_not((seg == half) & (kind == 0) & (t > 0)))
-                def _():
-                    arrived(relayed, place, u)
-                both_ways(relayed, u)
+        ahead = encoder & (kind == 0) & (t > 0) & ((seg == 0) | (t > 1))
+
+        @pl.when(decoder & jnp.logical_not(solo | ((idx > 0) & went_early(idx - 1))))
+        def _():
+            relay_own(idx)
+            relay_others(idx)
 
         @pl.when(active)
         def _():
-            for u in range(UNITS):
-                if u < OWN_UNITS:
-                    @pl.when(jnp.logical_not(local))
+            for u in range(OWN_UNITS):
+                @pl.when(jnp.logical_not(local | ahead))
+                def _():
+                    arrived(k, place, u)
+
+                @pl.when(jnp.logical_not(ahead | skip_held))
+                def _():
+                    send_near(k, u, False)
+
+                @pl.when(lends)
+                def _():
+                    across(k, place, u).start()
+                swap_after(k, place, u)
+
+            @pl.when(local | decoder)
+            def _():
+                for u in range(OWN_UNITS, UNITS):
+                    @pl.when(jnp.logical_not(local | skip_held))
                     def _():
                         arrived(k, place, u)
 
-                    @pl.when(jnp.logical_not(ahead | skip_held))
-                    def _():
-                        both_ways(k, u)
-
-                    @pl.when(lends)
+                    @pl.when((decoder & jnp.logical_not(skip_held)) | (encoder & solo))
+                    def _():
+                        send_near(k, u, False)
+
+                    @pl.when(lifts)
                     def _():
                         across(k, place, u).start()
-                else:
-                    @pl.when(jnp.logical_not(local | skip_held))
-                    def _():
-                        arrived(k, place, u)
-
-                    @pl.when(decoder & jnp.logical_not(skip_held))
-                    def _():
-                        both_ways(k, u)
-
-                    @pl.when(lifts)
-                    def _():
-                        across(k, place, u).start()
-                swap_after(k, place, u)
+                    swap_after(k, place, u)
+
+            @pl.when(encoder & (kind == 1) & facts_of(jnp.maximum(idx - 1, 0))[5])
+            def _():
+                q = source_of(others - 1)
+                for u in range(UNITS):
+                    if u < OWN_UNITS:
+                        across(k - 1, q, u).start()
+                    else:
+                        @pl.when(jnp.logical_not(twin_holds(q)))
+                        def _():
+                            across(k - 1, q, u).start()
 
             @pl.when(encoder | (kind == 0))
             def _():
                 acc[...] = jnp.zeros_like(acc)
 
-        @pl.when(idx > 0)
-        def _():
-            drain(idx - 1)
+        @pl.when(idx > 1)
+        def _():
+            drain(idx - 2)
 
         @pl.when(encoder & (idx == 0))
         def _():
@@ -447,13 +528,15 @@
             reload_taps(0, 9)
 
         def one_slot(s, _):
-            @pl.when(decoder & (s >= 1) & (s < length))
-            def _():
-                q = source_of(s - 1)
-                for u in range(OWN_UNITS, UNITS):
-                    arrived(relayed, q, u)
-                    onward(relayed, q, u)
-                    across(relayed, q, u).start()
+            @pl.when((idx < 2 * ticks - 2) & went_early(idx))
+            def _():
+                @pl.when(s == 3)
+                def _():
+                    relay_own(idx + 1)
+
+                @pl.when(s == 4)
+                def _():
+                    relay_others(idx + 1)
 
             e, part = event_of(jnp.maximum(s - 1, 0))
             gathers = active & (s >= 1) & (s <= 2 * others)
@@ -466,9 +549,9 @@
 
                     @pl.when(jnp.logical_not(skip_held))
                     def _():
-                        onward(k, q, u)
-
-                    @pl.when(lends)
+                        onward(k, q, u, False)
+
+                    @pl.when(lends & (e < others - 1))
                     def _():
                         across(k, q, u).start()
                     swap_after(k, q, u)
@@ -477,27 +560,43 @@
             def _():
                 q = source_of(e)
                 for u in range(OWN_UNITS, UNITS):
-                    @pl.when(jnp.logical_not(skip_held))
+                    @pl.when(jnp.logical_not(skip_held & twin_holds(q)))
                     def _():
                         arrived(k, q, u)
 
-                    @pl.when(decoder & jnp.logical_not(skip_held))
-                    def _():
-                        onward(k, q, u)
+                    @pl.when(lends & (e < others - 1) & jnp.logical_not(twin_holds(q)))
+                    def _():
+                        across(k, q, u).start()
+
+                    @pl.when((decoder & jnp.logical_not(skip_held)) | (encoder & solo))
+                    def _():
+                        onward(k, q, u, False)
                     swap_after(k, q, u)
 
-            @pl.when((seg == 0) & (kind == 1) & (t < ticks - 1) & (s == 2 * others - 1))
+            @pl.when(
+                encoder & (kind == 1) & (t < ticks - 1) & ((seg == 0) | (t > 0))
+                & (s == jnp.where(seg == 0, 2 * others - 1, slots - 1))
+            )
             def _():
                 for u in range(OWN_UNITS):
-                    both_ways(k + 1, u)
+                    @pl.when(seg > 0)
+                    def _():
+                        arrived(k + 1, place, u)
+                    send_near(k + 1, u, False)
+
+            @pl.when(encoder & jnp.logical_not(local) & (s == 1))
+            def _():
+                for u in range(OWN_UNITS, UNITS):
+                    arrived(k, place, u)
+                    swap_after(k, place, u)
+
+            @pl.when(encoder & (idx == 0) & (s >= 1) & (s < 4))
+            def _():
+                split_taps(1, 3 * s - 3, 3 * s)
 
             @pl.when((s >= third) & (s < third + 3))
             def _():
                 low = 3 * (s - third)
-
-                @pl.when(encoder & (idx == 0))
-                def _():
-                    split_taps(1, low, low + 3)
 
                 @pl.when(decoder & jnp.logical_not(merged) & (idx == 0))
                 def _():
@@ -519,14 +618,12 @@
                 q = jnp.where(s < 2, place, source_of(i))
                 h = jnp.where(s < 2, s, h)
 
-                @pl.when(h == 0)
-                def _():
-                    swap(k, 1 - core, q, 0).wait_recv()
-
-                @pl.when(h == 1)
-                def _():
-                    swap(k, 1 - core, q, 1).wait_recv()
-                    swap(k, 1 - core, q, 2).wait_recv()
+                for side in range(HALVES):
+                    @pl.when(h == side)
+                    def _():
+                        for part, (low, _) in enumerate(PARTS):
+                            if low // (UNITS // HALVES) == side:
+                                swap(k, 1 - core, q, part).wait_recv()
                 multiply(k, kind, q, h)
             return 0
         lax.fori_loop(0, slots, one_slot, 0)
@@ -600,20 +697,16 @@
             skip = skip & (mirror != half)
         if (segments + half) % 2 == 0:
             skip = skip & (mirror != shared)
+        mixed = sorted(range(UNITS), key=lambda u: (u % OWN_UNITS, u))
         if starting:
             @pl.when(helper)
             def _():
-                for u in range(OWN_UNITS, UNITS):
-                    give(t, 1, u, 1).start()
-
-            @pl.when(next_in)
-            def _():
-                for u in range(OWN_UNITS):
-                    give(t, 0, u, 1).start()
-
-            @pl.when(next_in)
-            def _():
-                for u in range(OWN_UNITS, UNITS):
+                for u in mixed:
+                    give(t, 0 if u < OWN_UNITS else 1, u, 1).start()
+
+            @pl.when(next_in & jnp.logical_not(helper))
+            def _():
+                for u in range(UNITS):
                     give(t, 0, u, 1).start()
 
             @pl.when(skip)
@@ -621,20 +714,22 @@
                 for u in range(UNITS):
                     give(t, 2, u, 1).start()
         else:
-            @pl.when(next_in)
+            @pl.when(helper)
+            def _():
+                give(t, 0, 0, OWN_UNITS).wait_send()
+                give(t, 1, OWN_UNITS, UNITS - OWN_UNITS).wait_send()
+
+            @pl.when(next_in & jnp.logical_not(helper))
             def _():
                 give(t, 0, 0, UNITS).wait_send()
 
-            @pl.when(helper)
-            def _():
-                give(t, 1, OWN_UNITS, UNITS - OWN_UNITS).wait_send()
-
             @pl.when(skip)
             def _():
                 give(t, 2, 0, UNITS).wait_send()
 
     lax.fori_loop(0, 2 * ticks, one_stage, 0)
-    drain(2 * ticks - 1)
+    for idx in range(max(0, 2 * ticks - 2), 2 * ticks):
+        drain(idx)
 
     for t in range(ticks - 1):
         @pl.when(encoder | decoder_active(seg, t))

time: 156 us -> 153 us (0.981)
  Pallas kernels: 153 us -> 151 us
    pallas_call x1, Pallas kernels: 153 us -> 151 us  [body(): pl.pallas_call(functools.partial(kernel, segments, n, ticks), out_shape=j...]
where the time goes in v2:
time: 153 us; the launch traced here: 152 us
  Pallas kernels  151 us (99%)
  local copies, waits for them, and re-layouts  1.72 us (1%)
    pallas_call x1, Pallas kernels, body(): pl.pallas_call(functools.partial(kernel, segments, n, ticks), out_shape=j...  151 us

profile of v2, /device:TPU:3, one launch (start us, length us, event | category | flops | bytes accessed | tf_op | source)
XLA Modules:
  0.0 152.5 jit_solution(13652381336052619248)
XLA Ops:
  0.0 150.8 %shard_map.55 = f32[160,512]{1,0:T(8,128)} custom-call(f32[160,512]{1,0:T(8,128)} %bitcast.4, f32[160,512]{1,0:T(8,128)} %bitcast.5, f32[2,160,512]{2,1,0:T(8,128)} %fresh.1, f32[1,160,11520]{2,1,0:T(8,128)} %first_weight.1, f32[1,160,11520]{2,1,0:T(8,128)} %second_weight.1), custom_call_target="tpu_custom_call" | custom-call | tf_op jit(solution)/shard_map/pallas_call | solution.py:748
  150.8 1.7 %copy.7 = f32[1,160,512]{2,1,0:T(8,128)} copy(f32[1,160,512]{2,1,0:T(8,128)} %bitcast.3) | data formatting | bytes 655360

commit v3 on v2

--- a/solution.py
+++ b/solution.py
@@ -21,13 +21,6 @@
 
 def silu(v):
     return v / (1.0 + jnp.exp(-v))
-
-
-def block_of(rows):
-    for size in (32, 40, 16):
-        if rows % size == 0:
-            return size
-    return 8
 
 
 def first_decoder_tick(segments, ticks):
@@ -57,8 +50,7 @@
     piece = positions // CHUNKS
     width = 2 * rows
     channels = length * width
-    blk = block_of(rows)
-    split_blk = 32 if rows % 32 == 0 else rows
+    blk = rows
     twin = jnp.where(encoder, seg + half, seg - half)
 
     def load(conv, tap, slot):
@@ -67,20 +59,14 @@
         return pltpu.make_async_copy(source.at[0, :, columns], stage.at[slot], w_sem.at[slot])
 
     def store_split(conv, tap, value_of):
-        def some_rows(i, _):
-            start = i * split_blk
-            if split_blk != rows:
-                start = pl.multiple_of(start, 16)
-            spot = pl.ds(pl.multiple_of(tap * rows + start, 16), split_blk)
-            for q in range(length):
-                value = value_of(pl.ds(start, split_blk), slice(q * width, (q + 1) * width))
-                high = value.astype(jnp.bfloat16)
-                low = (value - high.astype(jnp.float32)).astype(jnp.bfloat16)
-                wv[conv, q, spot, 0:width] = high
-                wv[conv, q, spot, width : 2 * width] = low
-                wv[conv, q, spot, 2 * width : 3 * width] = high
-            return 0
-        lax.fori_loop(0, rows // split_blk, some_rows, 0)
+        spot = pl.ds(pl.multiple_of(tap * rows, 16 if rows % 16 == 0 else 8), rows)
+        for q in range(length):
+            value = value_of(slice(q * width, (q + 1) * width))
+            high = value.astype(jnp.bfloat16)
+            low = (value - high.astype(jnp.float32)).astype(jnp.bfloat16)
+            wv[conv, q, spot, 0:width] = high
+            wv[conv, q, spot, width : 2 * width] = low
+            wv[conv, q, spot, 2 * width : 3 * width] = high
 
     depth = 4
 
@@ -102,7 +88,7 @@
     def split_taps(conv, low, high):
         def one(tap, _):
             load(0, 0, tap).wait()
-            store_split(conv, tap, lambda r, c: stage[tap, r, c])
+            store_split(conv, tap, lambda c: stage[tap, :, c])
             return 0
         lax.fori_loop(low, high, one, 0)
 
@@ -117,7 +103,7 @@
             a = tap % depth
             load(0, 0, a).wait()
             load(1, 0, depth + a).wait()
-            store_split(0, tap, lambda r, c: stage[a, r, c] + stage[depth + a, r, c])
+            store_split(0, tap, lambda c: stage[a, :, c] + stage[depth + a, :, c])
 
             @pl.when(tap + depth < 9)
             def _():

time: 153 us -> 146 us (0.954)
  Pallas kernels: 151 us -> 144 us
    pallas_call x1, Pallas kernels: 151 us -> 144 us  [body(): pl.pallas_call(functools.partial(kernel, segments, n, ticks), out_shape=j...]
where the time goes in v3:
time: 146 us
  Pallas kernels  144 us (99%)
  local copies, waits for them, and re-layouts  1.72 us (1%)
    pallas_call x1, Pallas kernels, body(): pl.pallas_call(functools.partial(kernel, segments, n, ticks), out_shape=j...  144 us

profile of v3, /device:TPU:3, one launch (start us, length us, event | category | flops | bytes accessed | tf_op | source)
XLA Modules:
  0.0 145.5 jit_solution(4458382992460410389)
XLA Ops:
  0.0 143.8 %shard_map.55 = f32[160,512]{1,0:T(8,128)} custom-call(f32[160,512]{1,0:T(8,128)} %bitcast.4, f32[160,512]{1,0:T(8,128)} %bitcast.5, f32[2,160,512]{2,1,0:T(8,128)} %fresh.1, f32[1,160,11520]{2,1,0:T(8,128)} %first_weight.1, f32[1,160,11520]{2,1,0:T(8,128)} %second_weight.1), custom_call_target="tpu_custom_call" | custom-call | tf_op jit(solution)/shard_map/pallas_call | solution.py:734
  143.8 1.7 %copy.7 = f32[1,160,512]{2,1,0:T(8,128)} copy(f32[1,160,512]{2,1,0:T(8,128)} %bitcast.3) | data formatting | bytes 655360

commit v4 on v3

--- a/solution.py
+++ b/solution.py
@@ -450,7 +450,7 @@
     def one_stage(idx, _):
         t, kind, k, active, lifts, lends, solo, skip_held = facts_of(idx)
         local = jnp.where(encoder, (kind == 1) | (t == 0) | (seg == 0), t == 0)
-        ahead = encoder & (kind == 0) & (t > 0) & ((seg == 0) | (t > 1))
+        ahead = encoder & (kind == 0) & (t > 0) & (seg == 0)
 
         @pl.when(decoder & jnp.logical_not(solo | ((idx > 0) & went_early(idx - 1))))
         def _():
@@ -560,14 +560,10 @@
                     swap_after(k, q, u)
 
             @pl.when(
-                encoder & (kind == 1) & (t < ticks - 1) & ((seg == 0) | (t > 0))
-                & (s == jnp.where(seg == 0, 2 * others - 1, slots - 1))
+                (seg == 0) & (kind == 1) & (t < ticks - 1) & (s == 2 * others - 1)
             )
             def _():
                 for u in range(OWN_UNITS):
-                    @pl.when(seg > 0)
-                    def _():
-                        arrived(k + 1, place, u)
                     send_near(k + 1, u, False)
 
             @pl.when(encoder & jnp.logical_not(local) & (s == 1))

time: 146 us -> 146 us (level)
  no operation moved by 1% of the time
where the time goes in v4:
time: 146 us
  Pallas kernels  144 us (99%)
  local copies, waits for them, and re-layouts  1.72 us (1%)
    pallas_call x1, Pallas kernels, body(): pl.pallas_call(functools.partial(kernel, segments, n, ticks), out_shape=j...  144 us

profile of v4, /device:TPU:3, one launch (start us, length us, event | category | flops | bytes accessed | tf_op | source)
XLA Modules:
  0.0 146.1 jit_solution(1408941237568923453)
XLA Ops:
  0.0 144.4 %shard_map.55 = f32[160,512]{1,0:T(8,128)} custom-call(f32[160,512]{1,0:T(8,128)} %bitcast.4, f32[160,512]{1,0:T(8,128)} %bitcast.5, f32[2,160,512]{2,1,0:T(8,128)} %fresh.1, f32[1,160,11520]{2,1,0:T(8,128)} %first_weight.1, f32[1,160,11520]{2,1,0:T(8,128)} %second_weight.1), custom_call_target="tpu_custom_call" | custom-call | tf_op jit(solution)/shard_map/pallas_call | solution.py:730
  144.4 1.7 %copy.7 = f32[1,160,512]{2,1,0:T(8,128)} copy(f32[1,160,512]{2,1,0:T(8,128)} %bitcast.3) | data formatting | bytes 655360
